TPU v7x, 256 devices: a whole 4x4x8 slice. The times are simulated.
256 devices in a mesh: blk: 32 (over x, z), leaf: 4 (over y), samp: 2 (over core).
Axes of the slice: x: 4, y: 4, z: 8, core: 2. Of those that a mesh axis runs over, the one named last changes fastest.
Arguments:
- points: float32 [3, 32768], P(None, ('blk', 'leaf')), may hold values from 0 to 64, as said below
- neighbors: int32 [128, 8], P(('blk', 'leaf')), may hold values from -1 to 127, as said below
- omega: float32 [512, 32768], P(None, ('blk', 'leaf')), may hold values from -6 to 6
- observed: float32 [32768], P(('blk', 'leaf')), may hold values from -6 to 6
- prior_draws: float32 [64, 32768], P('samp', ('blk', 'leaf')), may hold values from -6 to 6
Outputs:
- weights: float32 [64, 32768], P('samp', ('blk', 'leaf'))
- residual: float32 [64, 32768], P('samp', ('blk', 'leaf'))
Inputs may be any that keep to these rules, and one draw needn't show every extreme that they name: Block g's points lie in the unit cell with integer corner (cx, cy, cz), where cx // 2 = g // 4 and 0 <= cy, cz < 3. `neighbors`: row g lists in ascending order every block h whose unit cell touches g's (cells at most one apart in every coordinate, the first taken periodic of period 2 * 32), which includes every block with a point within distance 1 of a point of g, followed by -1 in the unused slots; the relation is symmetric, and every listed block has a slab index h // 4 equal to or cyclically next to g // 4.
All inputs are finite; a program needn't handle non-finite values.
Results may differ from a plain program's by a relative error of at most 0.0003.
Values sent between devices are 32-bit elements; how exact they have to be, the bound alone decides.
A program may use at most 64 MiB of HBM per device.

v0:
```python
import jax
import jax.numpy as jnp
from jax import lax
from jax.sharding import PartitionSpec as P

PB = 256
ITERS = 2
support_radius = 0.8
noise_variance = 1.0
sketch_shift = 1.0
ALL_AXES = ("blk", "leaf", "samp")


def shifted_2(block, axis, distance):
    devices = range(lax.axis_size(axis))
    route = [((i - distance) % len(devices), i) for i in devices]
    return lax.ppermute(block, axis, route)


def wendland(row_points, column_points, period):
    offset = row_points[None, :, :, None] - column_points[:, :, None, :]
    half_period = 0.5 * period
    along_x = jnp.mod(offset[:, 0] + half_period, period) - half_period
    squared = along_x * along_x + offset[:, 1] * offset[:, 1] + offset[:, 2] * offset[:, 2]
    radius = jnp.sqrt(squared) / support_radius
    remain = jnp.maximum(1.0 - radius, 0.0)
    return remain**4 * (4.0 * radius + 1.0)


def high_dot(left, right):
    return jnp.dot(left, right, precision=lax.Precision.HIGHEST, preferred_element_type=jnp.float32)


def shifted(values, offset_by):
    return shifted_2(values, "blk", offset_by)


def beside_all(values):
    slab_values = lax.all_gather(values, "leaf", axis=1, tiled=True)
    return jnp.concatenate([shifted(slab_values, 1), slab_values, shifted(slab_values, -1)], axis=1)


def lower_solve(factor, values):
    return lax.linalg.triangular_solve(factor, values, left_side=True, lower=True)


def local(points, neighbors, omega, observed, prior_draws):
    blk_dev = neighbors.shape[0]
    cycle_count = lax.axis_size("blk")
    slab_blocks = blk_dev * lax.axis_size("leaf")
    period = 2.0 * cycle_count
    own_slab = lax.axis_index("blk")
    n_samp = lax.axis_size("samp")
    samp_idx = lax.axis_index("samp")
    usable = neighbors >= 0
    relative = jnp.mod(neighbors // slab_blocks - own_slab + 1, cycle_count)
    chosen = jnp.where(usable, relative * slab_blocks + jnp.mod(neighbors, slab_blocks), 0)
    usable_weight = usable.astype(jnp.float32)
    reach_points = beside_all(points)
    reach_blocks = reach_points.reshape(3, 3 * slab_blocks, PB).transpose(1, 0, 2)
    row_blocks = points.reshape(3, blk_dev, PB).transpose(1, 0, 2)
    kernel_tile = wendland(row_blocks[0], reach_blocks[chosen[0]], period)
    kernel_tile = kernel_tile * usable_weight[0][:, None, None]

    def apply_kernel(values):
        width = values.shape[0]
        reach = beside_all(values).reshape(width, 3 * slab_blocks, PB)
        picked = jnp.take(reach, chosen[0], axis=1)
        return jnp.einsum("cnj,nij->ci", picked, kernel_tile, precision=lax.Precision.HIGHEST)

    def slot(x):
        zeros = jnp.zeros((n_samp,) + x.shape, x.dtype)
        return lax.dynamic_update_index_in_dim(zeros, x, samp_idx, 0)

    def unslot(xs):
        return lax.dynamic_index_in_dim(xs, samp_idx, 0, keepdims=False)

    def total_per_samp(values):
        return jax.tree.map(unslot, lax.psum(jax.tree.map(slot, values), ALL_AXES))

    sketch = apply_kernel(omega) + sketch_shift * omega
    rhs = observed[None, :] - prior_draws
    half = PB // n_samp
    omega_half = lax.dynamic_slice_in_dim(omega, samp_idx * half, half, axis=1)
    sketch_half = lax.dynamic_slice_in_dim(sketch, samp_idx * half, half, axis=1)
    core_part = high_dot(omega_half, sketch_half.T)
    square_part = high_dot(sketch_half, sketch_half.T)
    joint_part = 0.5 * (core_part + core_part.T) + 0.5 * (square_part + square_part.T)
    rhs_part = slot(high_dot(sketch, rhs.T))
    joint_gram, rhs_proj = lax.psum((joint_part, rhs_part), ALL_AXES)
    rhs_proj = unslot(rhs_proj)
    joint_factor = jnp.linalg.cholesky(joint_gram)

    def precond_from(vectors, projected):
        first_solve = lower_solve(joint_factor, projected)
        solved = lax.linalg.triangular_solve(
            joint_factor, first_solve, left_side=True, lower=True, transpose_a=True
        )
        return (vectors - high_dot(solved.T, sketch)) / noise_variance

    residual = rhs
    projected = rhs_proj
    precond = precond_from(residual, projected)
    direction = precond
    weights = jnp.zeros_like(rhs)
    image = apply_kernel(direction) + noise_variance * direction
    inner_now, curvature, image_proj = total_per_samp(
        (
            jnp.sum(residual * precond, axis=1),
            jnp.sum(direction * image, axis=1),
            high_dot(sketch, image.T),
        )
    )
    step_size = inner_now / curvature
    weights = weights + step_size[:, None] * direction
    residual = residual - step_size[:, None] * image
    projected = projected - step_size[None, :] * image_proj
    precond = precond_from(residual, projected)
    inner_next = total_per_samp(jnp.sum(residual * precond, axis=1))
    direction = precond + (inner_next / inner_now)[:, None] * direction
    inner_now = inner_next
    image = apply_kernel(direction) + noise_variance * direction
    curvature = total_per_samp(jnp.sum(direction * image, axis=1))
    step_size = inner_now / curvature
    weights = weights + step_size[:, None] * direction
    residual = residual - step_size[:, None] * image
    return (weights, residual)


def solution(mesh):
    in_specs = (
        P(None, ("blk", "leaf")),
        P(("blk", "leaf"), None),
        P(None, ("blk", "leaf")),
        P(("blk", "leaf")),
        P("samp", ("blk", "leaf")),
    )
    out_specs = (P("samp", ("blk", "leaf")), P("samp", ("blk", "leaf")))
    return jax.shard_map(local, mesh=mesh, in_specs=in_specs, out_specs=out_specs, check_vma=False)
```

profile of v0, /device:TPU:1, one launch (start us, length us, event | category | flops | bytes accessed | tf_op | source)
XLA Modules:
  0.0 1005.4 jit_solution(9335899095662480256)
XLA Ops:
  7.2 2.0 copy.10
  9.3 10.5 %all_gather.13 = f32[3,1024]{1,0:T(4,128)S(1)} all-gather(f32[3,256]{1,0:T(4,128)} %param.11), channel_id=1, replica_groups=mesh['blk'=32,'leaf'=4,'samp'=2] {'leaf'}, dimensions={1}, use_global_device_ids=true | all-gather | bytes 15360 | tf_op jit(solution)/shard_map/all_gather | solution.py:39
  19.9 7.8 collective-permute-start.3
  27.6 19.4 %all-gather.2.cloned.1.call-done = f32[512,1024]{0,1:T(8,128)} async-done(((f32[512,256]{0,1:T(8,128)}), f32[512,1024]{0,1:T(8,128)}) %all-gather.2.cloned.1.call-update) | async-done | bytes 2097168 | tf_op jit(solution)/shard_map/all_gather | solution.py:39
  47.1 5.2 collective-permute-start.1
  55.7 2.6 multiply_multiply_fusion
  58.3 38.5 %collective-permute-done.1 = f32[512,1024]{0,1:T(8,128)} collective-permute-done((f32[512,1024]{0,1:T(8,128)}, f32[512,1024]{0,1:T(8,128)}, u32[]{:S(2)}, u32[]{:S(2)}) %collective-permute-start.1) | collective-permute-done | bytes 2097184 | tf_op jit(solution)/shard_map/ppermute | solution.py:17
  96.8 5.4 collective-permute-done
  102.2 5.6 pad_maximum_fusion
  107.8 6.5 copy.11
  114.3 5.6 gather_fusion
  119.9 5.5 fusion.17
  125.4 2.0 fusion.34
  127.3 2.0 fusion.32
  129.4 2.5 copy.13
  131.9 2.5 copy.14
  134.5 3.7 fusion.26
  139.7 250.3 %all-reduce.8.cloned.1.call-done = (f32[512,512]{1,0:T(8,128)}, f32[2,512,32]{1,2,0:T(8,128)}) async-done(((f32[512,512]{1,0:T(8,128)}, f32[2,512,32]{1,2,0:T(8,128)}), (f32[512,512]{1,0:T(8,128)}, f32[2,512,32]{1,2,0:T(8,128)})) %all-reduce.8.cloned.1.call-update) | async-done | bytes 1179664 | tf_op jit(solution)/shard_map/psum | solution.py:90
  390.8 2.6 copy.15
  393.4 1.8 fusion.24
  396.2 11.7 %cholesky.104 = f32[128,128]{1,0:T(8,128)S(1)} custom-call(f32[128,128]{1,0:T(8,128)S(1)} %cholesky.266), custom_call_target="Cholesky" | custom-call | tf_op jit(solution)/shard_map/jit(cholesky)/cholesky | solution.py:92
  407.9 9.8 custom-call.33
  418.9 2.0 constant_dynamic-update-slice_fusion
  422.1 11.7 %cholesky.217 = f32[128,128]{1,0:T(8,128)S(1)} custom-call(f32[128,128]{1,0:T(8,128)S(1)} %cholesky.270), custom_call_target="Cholesky" | custom-call | tf_op jit(solution)/shard_map/jit(cholesky)/cholesky | solution.py:92
  434.5 10.2 %custom-call.34 = f32[1,128,128]{1,2,0:T(8,128)S(1)} custom-call(f32[1,128,128]{2,1,0:T(8,128)S(1)} %get-tuple-element.61), custom_call_target="InvertDiagBlocksLowerTriangular" | custom-call | tf_op jit(solution)/shard_map/jit(cholesky)/cholesky | solution.py:92
  447.1 11.7 %cholesky.238 = f32[128,128]{1,0:T(8,128)S(1)} custom-call(f32[128,128]{1,0:T(8,128)S(1)} %cholesky.275), custom_call_target="Cholesky" | custom-call | tf_op jit(solution)/shard_map/jit(cholesky)/cholesky | solution.py:92
  460.2 9.8 custom-call.35
  472.3 11.7 %cholesky.255 = f32[128,128]{1,0:T(8,128)S(1)} custom-call(f32[128,128]{1,0:T(8,128)S(1)} %convolution_subtract_fusion.2), custom_call_target="Cholesky" | custom-call | tf_op jit(solution)/shard_map/jit(cholesky)/cholesky | solution.py:92
  488.6 2.5 select_select_fusion
  491.1 12.0 %while.8 = (s32[]{:T(128)}, f32[512,512]{1,0:T(8,128)}, s32[4,2]{0,1:T(2,128)S(1)}, f32[4,128,128]{2,1,0:T(8,128)S(1)}, s32[]{:T(128)}) while((s32[]{:T(128)}, f32[512,512]{1,0:T(8,128)}, s32[4,2]{0,1:T(2,128)S(1)}, f32[4,128,128]{2,1,0:T(8,128)S(1)}, s32[]{:T(128)}) %tuple.51), condition=%wide.while_cond.1, body=%wide.while_body.1.sunk | while | flops 2 | bytes 131189 | solution.py:96
  491.7 2.3 bitcast_dynamic-update-slice_fusion.2
  494.8 2.3 bitcast_dynamic-update-slice_fusion.2
  497.8 2.3 bitcast_dynamic-update-slice_fusion.2
  500.8 2.3 bitcast_dynamic-update-slice_fusion.2
  503.1 39.3 %custom-call.39 = f32[4,128,128]{1,2,0:T(8,128)S(1)} custom-call(f32[4,128,128]{2,1,0:T(8,128)S(1)} %get-tuple-element.34), custom_call_target="InvertDiagBlocksLowerTriangular" | custom-call | tf_op jit(solution)/shard_map/triangular_solve/custom-call.8 | solution.py:96
  551.2 9.2 all_gather.14
  560.4 5.0 collective-permute-start.5
  565.4 1.9 collective-permute-done.5
  567.4 5.2 collective-permute-done.4
  573.2 2.8 multiply_reduce_fusion.3
  577.5 76.1 %all-reduce.1 = (f32[2,32]{1,0:T(2,128)S(1)}, f32[2,32]{1,0:T(2,128)S(1)}) all-reduce(f32[2,32]{1,0:T(2,128)S(1)} %dynamic_update_slice.22, f32[2,32]{1,0:T(2,128)S(1)} %dynamic_update_slice.21), channel_id=1, replica_groups=mesh['blk'=32,'leaf'=4,'samp'=2] {'blk','leaf','samp'}, use_global_device_ids=true, to_apply=%region_13.17 | all-reduce | flops 128 | bytes 1024 | tf_op jit(solution)/shard_map/psum | solution.py:79
  653.7 161.9 %all-reduce.6.cloned.1.call-done = f32[2,512,32]{1,2,0:T(8,128)} async-done(((f32[2,512,32]{1,2,0:T(8,128)}), f32[2,512,32]{1,2,0:T(8,128)}) %all-reduce.6.cloned.1.call-update) | async-done | bytes 131088 | tf_op jit(solution)/shard_map/psum | solution.py:79
  825.4 75.9 %psum.54 = f32[2,32]{1,0:T(2,128)S(1)} all-reduce(f32[2,32]{1,0:T(2,128)S(1)} %dynamic_update_slice.24), channel_id=1, replica_groups=mesh['blk'=32,'leaf'=4,'samp'=2] {'blk','leaf','samp'}, use_global_device_ids=true, to_apply=%region_16.20 | all-reduce | flops 64 | bytes 512 | tf_op jit(solution)/shard_map/psum | solution.py:79
  901.4 9.1 all_gather.15
  912.1 2.4 collective-permute-done.7
  914.5 4.6 collective-permute-done.6
  919.7 2.0 multiply_reduce_fusion
  921.8 76.2 %psum.55 = f32[2,32]{1,0:T(2,128)S(1)} all-reduce(f32[2,32]{1,0:T(2,128)S(1)} %dynamic_update_slice.25), channel_id=1, replica_groups=mesh['blk'=32,'leaf'=4,'samp'=2] {'blk','leaf','samp'}, use_global_device_ids=true, to_apply=%region_18.22 | all-reduce | flops 64 | bytes 512 | tf_op jit(solution)/shard_map/psum | solution.py:79
  (128 shorter events, 44.1 us)
Async XLA Ops:
  7.2 39.9 %all-gather.2.cloned.1.call-start = ((), (), s32[]{:S(2)}) async-start(), calls=%async_computation | async-start | bytes 2621440 | tf_op jit(solution)/shard_map/all_gather | solution.py:39
  9.3 380.7 %all-reduce.8.cloned.1.call-start = ((), (), s32[]{:S(2)}) async-start(), calls=%async_computation.2 | async-start | bytes 2359296 | tf_op jit(solution)/shard_map/psum | solution.py:90
  19.9 33.9 %collective-permute-start.3 = (f32[3,1024]{1,0:T(4,128)S(1)}, f32[3,1024]{1,0:T(4,128)S(1)}, u32[]{:S(2)}, u32[]{:S(2)}) collective-permute-start(f32[3,1024]{1,0:T(4,128)S(1)} %all_gather.13), channel_id=1, source_target_pairs={{8,0},{16,8},{24,16},{32,24},{40,32},{48,40},{56,48},{64,56},{72,6... | collective-permute-start | bytes 36872 | tf_op jit(solution)/shard_map/ppermute | solution.py:17
  27.6 26.1 %collective-permute-start.2 = (f32[3,1024]{1,0:T(4,128)S(1)}, f32[3,1024]{1,0:T(4,128)S(1)}, u32[]{:S(2)}, u32[]{:S(2)}) collective-permute-start(f32[3,1024]{1,0:T(4,128)S(1)} %all_gather.13), channel_id=1, source_target_pairs={{248,0},{0,8},{8,16},{16,24},{24,32},{32,40},{40,48},{48,56},{56,6... | collective-permute-start | bytes 36872 | tf_op jit(solution)/shard_map/ppermute | solution.py:17
  47.1 49.8 %collective-permute-start.1 = (f32[512,1024]{0,1:T(8,128)}, f32[512,1024]{0,1:T(8,128)}, u32[]{:S(2)}, u32[]{:S(2)}) collective-permute-start(f32[512,1024]{0,1:T(8,128)} %all-gather.2.cloned.1.call-done), channel_id=1, source_target_pairs={{8,0},{16,8},{24,16},{32,24},{40,32},{48,40},{56,48},{64,56},{72,6... | collective-permute-start | bytes 6291464 | tf_op jit(solution)/shard_map/ppermute | solution.py:17
  52.2 50.0 %collective-permute-start = (f32[512,1024]{0,1:T(8,128)}, f32[512,1024]{0,1:T(8,128)}, u32[]{:S(2)}, u32[]{:S(2)}) collective-permute-start(f32[512,1024]{0,1:T(8,128)} %all-gather.2.cloned.1.call-done), channel_id=1, source_target_pairs={{248,0},{0,8},{8,16},{16,24},{24,32},{32,40},{40,48},{48,56},{56,6... | collective-permute-start | bytes 6291464 | tf_op jit(solution)/shard_map/ppermute | solution.py:17
  55.7 46.5 %copy-start.2 = (f32[512,1024]{0,1:T(8,128)S(1)}, f32[512,1024]{0,1:T(8,128)}, u32[]{:S(2)}) copy-start(f32[512,1024]{0,1:T(8,128)} %all-gather.2.cloned.1.call-done) | copy-start | bytes 6291460
  114.3 5.6 copy-start
  134.5 3.7 copy-start.5
  134.5 3.7 copy-start.10
  138.8 0.6 copy-start.7
  139.4 676.2 %all-reduce.6.cloned.1.call-start = ((), (), s32[]{:S(2)}) async-start(), calls=%async_computation.1 | async-start | bytes 262144 | tf_op jit(solution)/shard_map/psum | solution.py:79
  395.2 1.0 copy-start.1
  551.2 16.2 %copy-start.3 = (f32[32,256]{1,0:T(8,128)}, f32[32,256]{1,0:T(8,128)S(1)}, u32[]{:S(2)}) copy-start(f32[32,256]{1,0:T(8,128)S(1)} %convolution_subtract_fusion.4) | copy-start | bytes 98308
  560.4 7.0 collective-permute-start.5
  565.4 7.1 collective-permute-start.4
  573.2 80.4 %copy-start.6 = (f32[32,256]{1,0:T(8,128)S(1)}, f32[32,256]{1,0:T(8,128)}, u32[]{:S(2)}) copy-start(f32[32,256]{1,0:T(8,128)} %param.15) | copy-start | bytes 98308
  573.2 242.4 %copy-start.9 = (f32[2,512,32]{1,2,0:T(8,128)S(1)}, f32[2,512,32]{1,2,0:T(8,128)}, u32[]{:S(2)}) copy-start(f32[2,512,32]{1,2,0:T(8,128)} %get-tuple-element.50) | copy-start | bytes 393220
  576.1 325.3 %copy-start.4 = (f32[32,256]{1,0:T(8,128)S(1)}, f32[32,256]{1,0:T(8,128)}, u32[]{:S(2)}) copy-start(f32[32,256]{1,0:T(8,128)} %copy-done.3) | copy-start | bytes 98308
  576.7 0.7 copy-start.8
  910.5 4.0 collective-permute-start.7
  911.9 7.1 collective-permute-start.6
Sparse Core Ops, SparseCore 0:
  9.8 37.2 all-gather.1
  139.5 250.3 all-reduce.7
  577.5 238.0 all-reduce.5
where the time goes:
time: 1010 us
  waiting for transfers between devices  490 us (49%)
  blocking collectives  257 us (25%)
  other arithmetic  141 us (14%)
  matrix products  40.6 us (4%)
  local copies, waits for them, and re-layouts  40.1 us (4%)
  starting transfers between devices  20.1 us (2%)
  between operations  17.2 us (2%)
    psum x1, waiting for transfers between devices, local(): joint_gram, rhs_proj = lax.psum((joint_part, rhs_part), ALL_AXES)  250 us
    psum x3, blocking collectives, total_per_samp(): return jax.tree.map(unslot, lax.psum(jax.tree.map(slot, values), ALL_AXES))  228 us
    psum x1, waiting for transfers between devices, total_per_samp(): return jax.tree.map(unslot, lax.psum(jax.tree.map(slot, values), ALL_AXES))  162 us
    another operation x14, other arithmetic, local(): joint_factor = jnp.linalg.cholesky(joint_gram)  80.7 us
    ppermute x8, waiting for transfers between devices, shifted_2(): return lax.ppermute(block, axis, route)  57.9 us
    another operation x4, other arithmetic, precond_from(): lax.linalg.triangular_solve(joint_factor, first_solve, left_side=True, lo...  41.8 us
    all_gather x3, blocking collectives, beside_all(): slab_values = lax.all_gather(values, 'leaf', axis=1, tiled=True)  28.8 us
  transfers between devices with their start and end apart: 11, of which 9 were waited for; matrix products, arithmetic and copies ran while one was open for 1% of the time, Pallas kernels for 0%

commit v1 on v0

--- a/solution.py
+++ b/solution.py
@@ -87,7 +87,8 @@
     square_part = high_dot(sketch_half, sketch_half.T)
     joint_part = 0.5 * (core_part + core_part.T) + 0.5 * (square_part + square_part.T)
     rhs_part = slot(high_dot(sketch, rhs.T))
-    joint_gram, rhs_proj = lax.psum((joint_part, rhs_part), ALL_AXES)
+    _produce_view = lambda peer_axis, xx, mesh_dim: lax.psum(lax.psum(xx, mesh_dim), peer_axis)
+    joint_gram, rhs_proj = _produce_view(("leaf", "samp"), (joint_part, rhs_part), "blk")
     rhs_proj = unslot(rhs_proj)
     joint_factor = jnp.linalg.cholesky(joint_gram)
 

time: 1010 us -> 971 us (0.961)
  waiting for transfers between devices: 490 us -> 449 us
    psum x1 -> x2, waiting for transfers between devices: 250 us -> 210 us  [the longest x1 139 us: local(): lax.psum(xx, mesh_dim)]
  transfers between devices with their start and end apart: 11 -> 12, of which waited for: 9 -> 10; matrix products, arithmetic and copies ran while one was open for 1% -> 1% of each run, Pallas kernels for 0% -> 0%
where the time goes in v1:
time: 971 us; the launch traced here: 967 us
  waiting for transfers between devices  449 us (46%)
  blocking collectives  259 us (27%)
  other arithmetic  141 us (15%)
  matrix products  40.6 us (4%)
  local copies, waits for them, and re-layouts  40 us (4%)
  starting transfers between devices  20.3 us (2%)
  between operations  17.2 us (2%)
    psum x3, blocking collectives, total_per_samp(): return jax.tree.map(unslot, lax.psum(jax.tree.map(slot, values), ALL_AXES))  229 us
    psum x1, waiting for transfers between devices, total_per_samp(): return jax.tree.map(unslot, lax.psum(jax.tree.map(slot, values), ALL_AXES))  162 us
    psum x1, waiting for transfers between devices, local(): lax.psum(xx, mesh_dim)  139 us
    another operation x14, other arithmetic, local(): joint_factor = jnp.linalg.cholesky(joint_gram)  80.7 us
    psum x1, waiting for transfers between devices, local(): lax.psum(lax.psum(xx, mesh_dim), peer_axis)  70.2 us
    ppermute x8, waiting for transfers between devices, shifted_2(): return lax.ppermute(block, axis, route)  57.9 us
    another operation x4, other arithmetic, precond_from(): lax.linalg.triangular_solve(joint_factor, first_solve, left_side=True, lo...  41.8 us
    all_gather x3, blocking collectives, beside_all(): slab_values = lax.all_gather(values, 'leaf', axis=1, tiled=True)  29.6 us
  transfers between devices with their start and end apart: 12, of which 10 were waited for; matrix products, arithmetic and copies ran while one was open for 1% of the time, Pallas kernels for 0%

profile of v1, /device:TPU:1, one launch (start us, length us, event | category | flops | bytes accessed | tf_op | source)
XLA Modules:
  0.0 966.7 jit_solution(11207303951882600330)
XLA Ops:
  7.2 2.0 copy.10
  9.3 10.5 %all_gather.13 = f32[3,1024]{1,0:T(4,128)S(1)} all-gather(f32[3,256]{1,0:T(4,128)} %param.11), channel_id=1, replica_groups=mesh['blk'=32,'leaf'=4,'samp'=2] {'leaf'}, dimensions={1}, use_global_device_ids=true | all-gather | bytes 15360 | tf_op jit(solution)/shard_map/all_gather | solution.py:39
  19.9 7.8 collective-permute-start.3
  27.6 19.4 %all-gather.2.cloned.1.call-done = f32[512,1024]{0,1:T(8,128)} async-done(((f32[512,256]{0,1:T(8,128)}), f32[512,1024]{0,1:T(8,128)}) %all-gather.2.cloned.1.call-update) | async-done | bytes 2097168 | tf_op jit(solution)/shard_map/all_gather | solution.py:39
  47.1 5.2 collective-permute-start.1
  55.7 2.6 multiply_multiply_fusion
  58.3 38.5 %collective-permute-done.1 = f32[512,1024]{0,1:T(8,128)} collective-permute-done((f32[512,1024]{0,1:T(8,128)}, f32[512,1024]{0,1:T(8,128)}, u32[]{:S(2)}, u32[]{:S(2)}) %collective-permute-start.1) | collective-permute-done | bytes 2097184 | tf_op jit(solution)/shard_map/ppermute | solution.py:17
  96.8 5.4 collective-permute-done
  102.2 5.6 pad_maximum_fusion
  107.8 6.5 copy.11
  114.3 5.6 gather_fusion
  119.9 5.5 fusion.17
  125.4 2.0 fusion.34
  127.3 2.0 fusion.32
  129.4 2.5 copy.13
  131.9 2.5 copy.14
  134.5 3.7 fusion.26
  139.5 139.4 %all-reduce.10.cloned.1.call-done = (f32[512,512]{1,0:T(8,128)}, f32[2,512,32]{1,2,0:T(8,128)}) async-done(((f32[512,512]{1,0:T(8,128)}, f32[2,512,32]{1,2,0:T(8,128)}), (f32[512,512]{1,0:T(8,128)}, f32[2,512,32]{1,2,0:T(8,128)})) %all-reduce.10.cloned.1.call-update) | async-done | bytes 1179664 | tf_op jit(solution)/shard_map/psum | solution.py:90
  279.2 70.2 %all-reduce.12.cloned.1.call-done = (f32[512,512]{1,0:T(8,128)}, f32[2,512,32]{1,2,0:T(8,128)}) async-done(((f32[512,512]{1,0:T(8,128)}, f32[2,512,32]{1,2,0:T(8,128)}), (f32[512,512]{1,0:T(8,128)}, f32[2,512,32]{1,2,0:T(8,128)})) %all-reduce.12.cloned.1.call-update) | async-done | bytes 1179664 | tf_op jit(solution)/shard_map/psum | solution.py:90
  350.2 2.5 copy.15
  355.5 11.7 %cholesky.104 = f32[128,128]{1,0:T(8,128)S(1)} custom-call(f32[128,128]{1,0:T(8,128)S(1)} %cholesky.266), custom_call_target="Cholesky" | custom-call | tf_op jit(solution)/shard_map/jit(cholesky)/cholesky | solution.py:93
  367.3 9.8 %custom-call.33 = f32[1,128,128]{1,2,0:T(8,128)S(1)} custom-call(f32[1,128,128]{2,1,0:T(8,128)S(1)} %get-tuple-element.66), custom_call_target="InvertDiagBlocksLowerTriangular" | custom-call | tf_op jit(solution)/shard_map/jit(cholesky)/cholesky | solution.py:93
  378.3 2.0 constant_dynamic-update-slice_fusion
  381.5 11.7 %cholesky.217 = f32[128,128]{1,0:T(8,128)S(1)} custom-call(f32[128,128]{1,0:T(8,128)S(1)} %cholesky.270), custom_call_target="Cholesky" | custom-call | tf_op jit(solution)/shard_map/jit(cholesky)/cholesky | solution.py:93
  393.9 10.2 %custom-call.34 = f32[1,128,128]{1,2,0:T(8,128)S(1)} custom-call(f32[1,128,128]{2,1,0:T(8,128)S(1)} %get-tuple-element.63), custom_call_target="InvertDiagBlocksLowerTriangular" | custom-call | tf_op jit(solution)/shard_map/jit(cholesky)/cholesky | solution.py:93
  406.5 11.7 %cholesky.238 = f32[128,128]{1,0:T(8,128)S(1)} custom-call(f32[128,128]{1,0:T(8,128)S(1)} %cholesky.275), custom_call_target="Cholesky" | custom-call | tf_op jit(solution)/shard_map/jit(cholesky)/cholesky | solution.py:93
  419.6 9.8 %custom-call.35 = f32[1,128,128]{1,2,0:T(8,128)S(1)} custom-call(f32[1,128,128]{2,1,0:T(8,128)S(1)} %get-tuple-element.60), custom_call_target="InvertDiagBlocksLowerTriangular" | custom-call | tf_op jit(solution)/shard_map/jit(cholesky)/cholesky | solution.py:93
  431.6 11.7 %cholesky.255 = f32[128,128]{1,0:T(8,128)S(1)} custom-call(f32[128,128]{1,0:T(8,128)S(1)} %convolution_subtract_fusion.2), custom_call_target="Cholesky" | custom-call | tf_op jit(solution)/shard_map/jit(cholesky)/cholesky | solution.py:93
  447.9 2.5 select_select_fusion
  450.4 12.0 %while.8 = (s32[]{:T(128)}, f32[512,512]{1,0:T(8,128)}, s32[4,2]{0,1:T(2,128)S(1)}, f32[4,128,128]{2,1,0:T(8,128)S(1)}, s32[]{:T(128)}) while((s32[]{:T(128)}, f32[512,512]{1,0:T(8,128)}, s32[4,2]{0,1:T(2,128)S(1)}, f32[4,128,128]{2,1,0:T(8,128)S(1)}, s32[]{:T(128)}) %tuple.51), condition=%wide.while_cond.1, body=%wide.while_body.1.sunk | while | flops 2 | bytes 131189 | solution.py:97
  451.1 2.3 bitcast_dynamic-update-slice_fusion.2
  454.1 2.3 bitcast_dynamic-update-slice_fusion.2
  457.2 2.3 bitcast_dynamic-update-slice_fusion.2
  460.2 2.3 bitcast_dynamic-update-slice_fusion.2
  462.5 39.3 %custom-call.39 = f32[4,128,128]{1,2,0:T(8,128)S(1)} custom-call(f32[4,128,128]{2,1,0:T(8,128)S(1)} %get-tuple-element.34), custom_call_target="InvertDiagBlocksLowerTriangular" | custom-call | tf_op jit(solution)/shard_map/triangular_solve/custom-call.8 | solution.py:97
  510.5 10.0 %all_gather.14 = f32[32,1024]{1,0:T(8,128)S(1)} all-gather(f32[32,256]{1,0:T(8,128)S(1)} %convolution_subtract_fusion.4), channel_id=1, replica_groups=mesh['blk'=32,'leaf'=4,'samp'=2] {'leaf'}, dimensions={1}, use_global_device_ids=true | all-gather | bytes 163840 | tf_op jit(solution)/shard_map/all_gather | solution.py:39
  520.6 5.2 collective-permute-start.5
  525.7 1.9 collective-permute-done.5
  527.7 5.2 collective-permute-done.4
  533.5 2.8 multiply_reduce_fusion.3
  537.8 77.2 %all-reduce.1 = (f32[2,32]{1,0:T(2,128)S(1)}, f32[2,32]{1,0:T(2,128)S(1)}) all-reduce(f32[2,32]{1,0:T(2,128)S(1)} %dynamic_update_slice.22, f32[2,32]{1,0:T(2,128)S(1)} %dynamic_update_slice.21), channel_id=1, replica_groups=mesh['blk'=32,'leaf'=4,'samp'=2] {'blk','leaf','samp'}, use_global_device_ids=true, to_apply=%region_15.19 | all-reduce | flops 128 | bytes 1024 | tf_op jit(solution)/shard_map/psum | solution.py:79
  615.0 161.8 %all-reduce.8.cloned.1.call-done = f32[2,512,32]{1,2,0:T(8,128)} async-done(((f32[2,512,32]{1,2,0:T(8,128)}), f32[2,512,32]{1,2,0:T(8,128)}) %all-reduce.8.cloned.1.call-update) | async-done | bytes 131088 | tf_op jit(solution)/shard_map/psum | solution.py:79
  786.7 75.9 %psum.70 = f32[2,32]{1,0:T(2,128)S(1)} all-reduce(f32[2,32]{1,0:T(2,128)S(1)} %dynamic_update_slice.24), channel_id=1, replica_groups=mesh['blk'=32,'leaf'=4,'samp'=2] {'blk','leaf','samp'}, use_global_device_ids=true, to_apply=%region_18.22 | all-reduce | flops 64 | bytes 512 | tf_op jit(solution)/shard_map/psum | solution.py:79
  862.7 9.1 all_gather.15
  873.5 2.4 collective-permute-done.7
  875.8 4.6 collective-permute-done.6
  881.0 2.0 multiply_reduce_fusion
  883.1 76.2 %psum.71 = f32[2,32]{1,0:T(2,128)S(1)} all-reduce(f32[2,32]{1,0:T(2,128)S(1)} %dynamic_update_slice.25), channel_id=1, replica_groups=mesh['blk'=32,'leaf'=4,'samp'=2] {'blk','leaf','samp'}, use_global_device_ids=true, to_apply=%region_20.24 | all-reduce | flops 64 | bytes 512 | tf_op jit(solution)/shard_map/psum | solution.py:79
  (129 shorter events, 45.9 us)
Async XLA Ops:
  7.2 39.9 %all-gather.2.cloned.1.call-start = ((), (), s32[]{:S(2)}) async-start(), calls=%async_computation | async-start | bytes 2621440 | tf_op jit(solution)/shard_map/all_gather | solution.py:39
  9.3 269.6 %all-reduce.10.cloned.1.call-start = ((), (), s32[]{:S(2)}) async-start(), calls=%async_computation.2 | async-start | bytes 2359296 | tf_op jit(solution)/shard_map/psum | solution.py:90
  19.9 33.9 %collective-permute-start.3 = (f32[3,1024]{1,0:T(4,128)S(1)}, f32[3,1024]{1,0:T(4,128)S(1)}, u32[]{:S(2)}, u32[]{:S(2)}) collective-permute-start(f32[3,1024]{1,0:T(4,128)S(1)} %all_gather.13), channel_id=1, source_target_pairs={{8,0},{16,8},{24,16},{32,24},{40,32},{48,40},{56,48},{64,56},{72,6... | collective-permute-start | bytes 36872 | tf_op jit(solution)/shard_map/ppermute | solution.py:17
  27.6 26.1 %collective-permute-start.2 = (f32[3,1024]{1,0:T(4,128)S(1)}, f32[3,1024]{1,0:T(4,128)S(1)}, u32[]{:S(2)}, u32[]{:S(2)}) collective-permute-start(f32[3,1024]{1,0:T(4,128)S(1)} %all_gather.13), channel_id=1, source_target_pairs={{248,0},{0,8},{8,16},{16,24},{24,32},{32,40},{40,48},{48,56},{56,6... | collective-permute-start | bytes 36872 | tf_op jit(solution)/shard_map/ppermute | solution.py:17
  47.1 49.8 %collective-permute-start.1 = (f32[512,1024]{0,1:T(8,128)}, f32[512,1024]{0,1:T(8,128)}, u32[]{:S(2)}, u32[]{:S(2)}) collective-permute-start(f32[512,1024]{0,1:T(8,128)} %all-gather.2.cloned.1.call-done), channel_id=1, source_target_pairs={{8,0},{16,8},{24,16},{32,24},{40,32},{48,40},{56,48},{64,56},{72,6... | collective-permute-start | bytes 6291464 | tf_op jit(solution)/shard_map/ppermute | solution.py:17
  52.2 50.0 %collective-permute-start = (f32[512,1024]{0,1:T(8,128)}, f32[512,1024]{0,1:T(8,128)}, u32[]{:S(2)}, u32[]{:S(2)}) collective-permute-start(f32[512,1024]{0,1:T(8,128)} %all-gather.2.cloned.1.call-done), channel_id=1, source_target_pairs={{248,0},{0,8},{8,16},{16,24},{24,32},{32,40},{40,48},{48,56},{56,6... | collective-permute-start | bytes 6291464 | tf_op jit(solution)/shard_map/ppermute | solution.py:17
  55.7 46.5 %copy-start.2 = (f32[512,1024]{0,1:T(8,128)S(1)}, f32[512,1024]{0,1:T(8,128)}, u32[]{:S(2)}) copy-start(f32[512,1024]{0,1:T(8,128)} %all-gather.2.cloned.1.call-done) | copy-start | bytes 6291460
  114.3 5.6 copy-start
  134.5 3.7 copy-start.5
  134.5 3.7 copy-start.9
  138.8 0.6 copy-start.7
  139.4 210.0 %all-reduce.12.cloned.1.call-start = ((), (), s32[]{:S(2)}) async-start(), calls=%async_computation.3 | async-start | bytes 2359296 | tf_op jit(solution)/shard_map/psum | solution.py:90
  278.9 498.0 %all-reduce.8.cloned.1.call-start = ((), (), s32[]{:S(2)}) async-start(), calls=%async_computation.1 | async-start | bytes 262144 | tf_op jit(solution)/shard_map/psum | solution.py:79
  354.5 1.0 copy-start.1
  510.5 17.2 %copy-start.3 = (f32[32,256]{1,0:T(8,128)}, f32[32,256]{1,0:T(8,128)S(1)}, u32[]{:S(2)}) copy-start(f32[32,256]{1,0:T(8,128)S(1)} %convolution_subtract_fusion.4) | copy-start | bytes 98308
  520.6 7.1 collective-permute-start.5
  525.7 7.1 collective-permute-start.4
  533.5 81.4 %copy-start.6 = (f32[32,256]{1,0:T(8,128)S(1)}, f32[32,256]{1,0:T(8,128)}, u32[]{:S(2)}) copy-start(f32[32,256]{1,0:T(8,128)} %param.15) | copy-start | bytes 98308
  536.4 326.3 %copy-start.4 = (f32[32,256]{1,0:T(8,128)S(1)}, f32[32,256]{1,0:T(8,128)}, u32[]{:S(2)}) copy-start(f32[32,256]{1,0:T(8,128)} %copy-done.3) | copy-start | bytes 98308
  537.0 0.7 copy-start.8
  871.8 4.0 collective-permute-start.7
  873.2 7.1 collective-permute-start.6
Sparse Core Ops, SparseCore 0:
  9.8 37.2 all-gather.1
  139.5 139.2 all-reduce.9
  281.3 67.9 all-reduce.11
  537.8 239.0 all-reduce.7
